TPU v7x, 32 devices: a whole 2x2x4 slice. The times are simulated.
32 devices in a mesh: fields: 2 (over x), prow: 8 (over z, y), pcol: 2 (over core).
Axes of the slice: x: 2, y: 2, z: 4, core: 2. Of those that a mesh axis runs over, the one named last changes fastest.
Arguments:
- inverse_tiles: bfloat16 [32, 16, 256, 256], P(('fields', 'prow'), 'pcol'), parts along dimension 0, may hold values from -6 to 6
- panel_blocks: bfloat16 [4, 8, 256, 512], P('fields', 'prow', None, 'pcol'), parts along dimension 0, may hold values from -0.125 to 0.125
- diag_inverse: float32 [4, 512], P('fields', 'pcol'), parts along dimension 0, may hold values from 0.5 to 2
- structure: int32 [4, 8], P('fields'), parts along dimension 0, may hold values from 0 to 15, as said below
- block_slot: int32 [32], P('fields'), parts along dimension 0, may hold values from 0 to 15, each once
Outputs:
- sigma_new: bfloat16 [4, 16, 256, 512], P('fields', 'prow', None, 'pcol'), parts along dimension 0
- variances: float32 [4, 512], P('fields', 'pcol'), parts along dimension 0
There are 2 independent parts, one for each index of `fields`. A program takes and returns all parts, laid end to end along the dimension named above; each array names one. Nothing has to cross between parts.
Inputs may be any that keep to these rules, and one draw needn't show every extreme that they name: `structure`: each row lists 8 distinct row blocks in increasing order, and the last is always 16 - 1. `block_slot`: each slot is used by exactly one row block.
All inputs are finite; a program needn't handle non-finite values.
Results may differ from a plain program's by a relative error of at most 0.0006.
Values may be sent and summed in bfloat16 or wider, within the bound.
No kernel may reach another device: no remote copies, remote signals or barrier semaphores. Data moves between devices by JAX's collectives and lax.ppermute only.
A program may use at most 128 MiB of HBM per device.

v0:
```python
import jax
import jax.numpy as jnp
from jax import lax
from jax.sharding import PartitionSpec as P


def swapped(shard, axis, stride):
    return lax.ppermute(shard, axis, [(i, i ^ 1 << stride) for i in range(lax.axis_size(axis))])


def make_accumulate(selected, row_hits, piece):
    contrib = jnp.einsum("iskxy,skyw->sixw", selected, piece, preferred_element_type=jnp.float32)
    own_panel = jnp.einsum("sik,skxw->sixw", row_hits, piece, preferred_element_type=jnp.float32)
    return (contrib, own_panel)


def per_device(inverse_tiles, panel_blocks, diag_inverse, structure, block_slot):
    rows_here = inverse_tiles.shape[0]
    tile_size = inverse_tiles.shape[2]
    supernodes = panel_blocks.shape[0]
    positions = structure.shape[1]
    prow_index = lax.axis_index("prow")
    pcol_index = lax.axis_index("pcol")
    slot_of = block_slot[structure]
    own_rows = prow_index * rows_here + jnp.arange(rows_here, dtype=jnp.int32)
    row_match = slot_of[:, None, :] == own_rows[None, :, None]
    row_hits = row_match.astype(jnp.bfloat16)
    row_used = jnp.any(row_match, axis=2)
    partner = swapped(inverse_tiles, "pcol", 0)
    first_half = jnp.where(pcol_index == 0, inverse_tiles, partner)
    second_half = jnp.where(pcol_index == 0, partner, inverse_tiles)
    whole_rows = jnp.concatenate([first_half, second_half], axis=1)
    selected = jnp.take(whole_rows, slot_of.reshape(-1), axis=1)
    selected = selected.reshape(rows_here, supernodes, positions, tile_size, tile_size)
    summed, own_panel = make_accumulate(
        selected, row_hits, lax.all_gather(panel_blocks, "prow", axis=1, tiled=True)
    )
    sigma_rows = jnp.where(row_used[:, :, None, None], -summed, jnp.zeros((), jnp.float32))
    partial_value = jnp.sum(own_panel * sigma_rows, axis=(1, 2))
    correction = lax.psum(partial_value, "prow")
    variances = diag_inverse - correction
    return (sigma_rows.astype(jnp.bfloat16), variances)


def solution(mesh):
    in_specs = (
        P(("fields", "prow"), "pcol", None, None),
        P("fields", "prow", None, "pcol"),
        P("fields", "pcol"),
        P("fields", None),
        P("fields"),
    )
    out_specs = (P("fields", "prow", None, "pcol"), P("fields", "pcol"))
    return jax.shard_map(
        per_device, mesh=mesh, in_specs=in_specs, out_specs=out_specs, check_vma=False
    )
```

profile of v0, /device:TPU:0, one launch (start us, length us, event | category | flops | bytes accessed | tf_op | source)
XLA Modules:
  0.0 95.9 jit_solution(17099047433927221169)
XLA Ops:
  7.2 0.0 copy-start
  7.2 0.0 all-gather.2.cloned.1.call-start
  7.2 0.7 all-gather.2.cloned.1.call-update
  7.9 0.6 collective-permute-start
  8.5 0.7 compare_select_fusion.1
  9.2 0.1 reshape.53
  9.2 0.0 copy-done
  9.2 0.7 gather_fusion
  9.9 0.1 reshape.52
  10.0 0.2 compare_reduce_fusion
  10.2 2.3 %collective-permute-done = bf16[2,8,256,256]{3,2,1,0:T(8,128)(2,1)S(1)} collective-permute-done((bf16[2,8,256,256]{3,2,1,0:T(8,128)(2,1)}, bf16[2,8,256,256]{3,2,1,0:T(8,128)(2,1)S(1)}, u32[]{:S(2)}, u32[]{:S(2)}) %collective-permute-start) | collective-permute-done | bytes 2097184 | tf_op jit(solution)/shard_map/ppermute | solution.py:8
  12.5 1.9 %broadcast_select_fusion.1 = (bf16[2,8,256,256]{3,2,1,0:T(8,128)(2,1)S(1)}, bf16[2,8,256,256]{3,2,1,0:T(8,128)(2,1)S(1)}) fusion(bf16[2,8,256,256]{3,2,1,0:T(8,128)(2,1)} %param.5, bf16[2,8,256,256]{3,2,1,0:T(8,128)(2,1)S(1)} %collective-permute-done, pred[]{:T(512)S(6)} %eq.20), kind=kLoop, calls=%fused_computation.11 | loop fusion | flops 2097152 | bytes 8388609 | tf_op jit(solution)/shard_map/jit(_where)/select_n | solution.py:30
  14.3 2.3 %pad_maximum_fusion = bf16[2,16,256,256]{3,2,1,0:T(8,128)(2,1)} fusion(bf16[2,8,256,256]{3,2,1,0:T(8,128)(2,1)S(1)} %get-tuple-element.3, bf16[2,8,256,256]{3,2,1,0:T(8,128)(2,1)S(1)} %get-tuple-element.2), kind=kLoop, calls=%fused_computation.2 | loop fusion | flops 2097152 | bytes 8388608 | tf_op jit(solution)/shard_map/concatenate | solution.py:32
  16.7 4.9 %gather_fusion.1 = bf16[16,2,256,256]{3,2,1,0:T(8,128)(2,1)} fusion(bf16[2,16,256,256]{3,2,1,0:T(8,128)(2,1)} %pad_maximum_fusion, s32[1024]{0:T(1024)S(1)} %pad_clamp_fusion), kind=kCustom, calls=%fused_computation.1 | custom fusion | bytes 8388672 | tf_op jit(solution)/shard_map/jit(_take)/gather | solution.py:33
  21.6 40.4 %all-gather.2.cloned.1.call-done = bf16[2,8,256,256]{3,2,1,0:T(8,128)(2,1)} async-done(((bf16[2,1,256,256]{3,2,1,0:T(8,128)(2,1)}), bf16[2,8,256,256]{3,2,1,0:T(8,128)(2,1)}) %all-gather.2.cloned.1.call-update) | async-done | bytes 2097168 | tf_op jit(solution)/shard_map/all_gather | solution.py:36
  62.0 0.0 copy-start.1
  62.0 3.2 %fusion.3 = f32[2,2,256,256]{3,1,2,0:T(2,128)S(1)} fusion(bf16[2,8,256,256]{3,2,1,0:T(8,128)(2,1)} %all-gather.2.cloned.1.call-done, s32[2,8]{1,0:T(2,128)S(1)} %reshape.52, s32[2]{0:T(128)S(1)} %iota_add_fusion), kind=kOutput, calls=%fused_computation.7 | convolution fusion | flops 4194336 | bytes 3145800 | tf_op jit(solution)/shard_map/sik,skxw->sixw/dot_general | solution.py:13
  65.2 0.0 copy-done.1
  65.2 0.0 copy-start.2
  65.2 4.3 %fusion.15 = (f32[2,256]{1,0:T(2,128)S(1)}, bf16[2,2,256,256]{3,2,1,0:T(8,128)(2,1)}) fusion(f32[2,2,256,256]{3,1,2,0:T(2,128)S(1)} %fusion.3, bf16[2,8,256,256]{3,2,1,0:T(8,128)(2,1)S(1)} %copy-done.1, bf16[2,2,8,256,256]{4,3,0,2,1:T(8,128)(2,1)} %bitcast.32, pred[2,8]{1,0:T(4,128)(4,1)S(1)} %compare_and_fusion, pred[2,2]{1,0:T(4,128)(4,1)S(1)} %compare_reduce_fusion), kind=kOutput, calls=%fused_computation.16 | convolution fusion | flops 1077149184 | bytes 7866388 | tf_op jit(solution)/shard_map/iskxy,skyw->sixw/dot_general | solution.py:12
  69.5 19.0 %psum.7 = f32[2,256]{1,0:T(2,128)S(1)} all-reduce(f32[2,256]{1,0:T(2,128)S(1)} %get-tuple-element.4), channel_id=1, replica_groups=mesh['fields'=2,'prow'=8,'pcol'=2] {'prow'}, use_global_device_ids=true, to_apply=%region_2.3 | all-reduce | flops 512 | bytes 4096 | tf_op jit(solution)/shard_map/psum | solution.py:40
  88.5 0.0 copy-done.2
  88.5 0.6 sub.3
  (5 shorter events, 0.0 us)
Async XLA Ops:
  7.2 2.1 %copy-start = (s32[16]{0:T(128)S(1)}, s32[16]{0:T(128)}, u32[]{:S(2)}) copy-start(s32[16]{0:T(128)} %param.9) | copy-start | bytes 196
  7.2 54.8 %all-gather.2.cloned.1.call-start = ((), (), s32[]{:S(2)}) async-start(), calls=%async_computation | async-start | bytes 2359296 | tf_op jit(solution)/shard_map/all_gather | solution.py:36
  7.9 4.6 %collective-permute-start = (bf16[2,8,256,256]{3,2,1,0:T(8,128)(2,1)}, bf16[2,8,256,256]{3,2,1,0:T(8,128)(2,1)S(1)}, u32[]{:S(2)}, u32[]{:S(2)}) collective-permute-start(bf16[2,8,256,256]{3,2,1,0:T(8,128)(2,1)} %param.5), channel_id=1, source_target_pairs={{0,1},{1,0},{2,3},{3,2},{4,5},{5,4},{6,7},{7,6},{8,9},{9,8},{10,11... | collective-permute-start | bytes 6291464 | tf_op jit(solution)/shard_map/ppermute | solution.py:8
  62.0 3.2 %copy-start.1 = (bf16[2,8,256,256]{3,2,1,0:T(8,128)(2,1)S(1)}, bf16[2,8,256,256]{3,2,1,0:T(8,128)(2,1)}, u32[]{:S(2)}) copy-start(bf16[2,8,256,256]{3,2,1,0:T(8,128)(2,1)} %all-gather.2.cloned.1.call-done) | copy-start | bytes 6291460
  65.2 23.3 %copy-start.2 = (f32[2,256]{1,0:T(2,128)S(1)}, f32[2,256]{1,0:T(2,128)}, u32[]{:S(2)}) copy-start(f32[2,256]{1,0:T(2,128)} %param.7) | copy-start | bytes 6148
Sparse Core Ops, SparseCore 0:
  10.2 51.7 all-gather.1
where the time goes:
time: 96.1 us; the launch traced here: 95.9 us
  waiting for transfers between devices  43.3 us (45%)
  blocking collectives  19 us (20%)
  between operations  14.1 us (15%)
  matrix products  7.51 us (8%)
  local copies, waits for them, and re-layouts  5.78 us (6%)
  other arithmetic  5.67 us (6%)
    all_gather x1, waiting for transfers between devices, per_device(): lax.all_gather(panel_blocks, 'prow', axis=1, tiled=True)  40.4 us
    psum x1, blocking collectives, per_device(): correction = lax.psum(partial_value, 'prow')  19 us
    gather x1, local copies, waits for them, and re-layouts, per_device(): selected = jnp.take(whole_rows, slot_of.reshape(-1), axis=1)  4.94 us
    dot_general x1, matrix products, make_accumulate(): jnp.einsum('iskxy,skyw->sixw', selected, piece, preferred_element_type=jn...  4.32 us
    dot_general x1, matrix products, make_accumulate(): jnp.einsum('sik,skxw->sixw', row_hits, piece, preferred_element_type=jnp....  3.19 us
    concatenate x1, other arithmetic, per_device(): whole_rows = jnp.concatenate([first_half, second_half], axis=1)  2.33 us
    ppermute x1, waiting for transfers between devices, swapped(): lax.ppermute(shard, axis, [(i, i ^ 1 << stride) for i in range(lax.axis_s...  2.26 us
  transfers between devices with their start and end apart: 2, of which 2 were waited for; matrix products, arithmetic and copies ran while one was open for 11% of the time, Pallas kernels for 0%

commit v1 on v0

--- a/solution.py
+++ b/solution.py
@@ -2,6 +2,28 @@
 import jax.numpy as jnp
 from jax import lax
 from jax.sharding import PartitionSpec as P
+
+
+def in_order(blocks, dim):
+    blocks = jnp.moveaxis(blocks, 0, dim)
+    shape = blocks.shape
+    return blocks.reshape(*shape[:dim], shape[dim] * shape[dim + 1], *shape[dim + 2 :])
+
+
+def doubled(value, axis):
+    count = lax.axis_size(axis)
+    parts = value[None]
+    for level in range(count.bit_length() - 1):
+        apart = 1 << level
+        other = lax.ppermute(parts, axis, [(i, i ^ apart) for i in range(count)])
+        both = jnp.stack([parts, other])
+        upper = lax.axis_index(axis) >> level & 1
+        parts = jnp.where(upper == 0, both, both[::-1]).reshape(-1, *value.shape)
+    return parts
+
+
+def collect(value, axis, dim):
+    return in_order(doubled(value, axis), dim)
 
 
 def swapped(shard, axis, stride):
@@ -32,9 +54,7 @@
     whole_rows = jnp.concatenate([first_half, second_half], axis=1)
     selected = jnp.take(whole_rows, slot_of.reshape(-1), axis=1)
     selected = selected.reshape(rows_here, supernodes, positions, tile_size, tile_size)
-    summed, own_panel = make_accumulate(
-        selected, row_hits, lax.all_gather(panel_blocks, "prow", axis=1, tiled=True)
-    )
+    summed, own_panel = make_accumulate(selected, row_hits, collect(panel_blocks, "prow", 1))
     sigma_rows = jnp.where(row_used[:, :, None, None], -summed, jnp.zeros((), jnp.float32))
     partial_value = jnp.sum(own_panel * sigma_rows, axis=(1, 2))
     correction = lax.psum(partial_value, "prow")

time: 96.1 us -> 110 us (1.14)
  waiting for transfers between devices: 43.3 us -> 61.1 us
  between operations: 14.1 us -> 0.69 us
  starting transfers between devices: 0.6 us -> 7.52 us
  blocking collectives: 19 us -> 21.2 us
  other arithmetic: 5.67 us -> 7.71 us
  matrix products: 7.51 us -> 5.76 us
    ppermute x0 -> x3, waiting for transfers between devices: none -> 61 us  [doubled(): other = lax.ppermute(parts, axis, [(i, i ^ apart) for i in range(count)])]
    all_gather x1 -> x0, waiting for transfers between devices: 40.4 us -> none  [per_device(): lax.all_gather(panel_blocks, 'prow', axis=1, tiled=True)]
    ppermute x0 -> x3, starting transfers between devices: none -> 7.52 us  [doubled(): other = lax.ppermute(parts, axis, [(i, i ^ apart) for i in range(count)])]
    ppermute x1, waiting for transfers between devices: 2.26 us -> 0.01 us  [swapped(): lax.ppermute(shard, axis, [(i, i ^ 1 << stride) for i in range(lax.axis_s...]
    psum x1, blocking collectives: 19 us -> 21.2 us  [per_device(): correction = lax.psum(partial_value, 'prow')]
    dot_general x1, matrix products: 3.19 us -> 1.45 us  [make_accumulate(): jnp.einsum('sik,skxw->sixw', row_hits, piece, preferred_element_type=jnp....]
    another operation x0 -> x4, other arithmetic: none -> 1.41 us  [doubled(): both = jnp.stack([parts, other])]
  transfers between devices with their start and end apart: 2 -> 4, of which waited for: 2 -> 3; matrix products, arithmetic and copies ran while one was open for 11% -> 3% of each run, Pallas kernels for 0% -> 0%
where the time goes in v1:
time: 110 us
  waiting for transfers between devices  61.1 us (56%)
  blocking collectives  21.2 us (19%)
  other arithmetic  7.71 us (7%)
  starting transfers between devices  7.52 us (7%)
  local copies, waits for them, and re-layouts  5.8 us (5%)
  matrix products  5.76 us (5%)
    ppermute x3, waiting for transfers between devices, doubled(): other = lax.ppermute(parts, axis, [(i, i ^ apart) for i in range(count)])  61 us
    psum x1, blocking collectives, per_device(): correction = lax.psum(partial_value, 'prow')  21.2 us
    ppermute x3, starting transfers between devices, doubled(): other = lax.ppermute(parts, axis, [(i, i ^ apart) for i in range(count)])  7.52 us
    gather x1, local copies, waits for them, and re-layouts, per_device(): selected = jnp.take(whole_rows, slot_of.reshape(-1), axis=1)  4.96 us
    dot_general x1, matrix products, make_accumulate(): jnp.einsum('iskxy,skyw->sixw', selected, piece, preferred_element_type=jn...  4.31 us
    select_n x1, other arithmetic, per_device(): first_half = jnp.where(pcol_index == 0, inverse_tiles, partner)  2.5 us
    concatenate x1, other arithmetic, per_device(): whole_rows = jnp.concatenate([first_half, second_half], axis=1)  2.3 us
  transfers between devices with their start and end apart: 4, of which 3 were waited for; matrix products, arithmetic and copies ran while one was open for 3% of the time, Pallas kernels for 0%

profile of v1, /device:TPU:0, one launch (start us, length us, event | category | flops | bytes accessed | tf_op | source)
XLA Modules:
  0.0 109.7 jit_solution(16270197471320280172)
XLA Ops:
  0.6 0.0 copy-start
  0.6 3.1 %collective-permute-start.1 = (bf16[1,2,1,256,256]{4,3,1,2,0:T(8,128)(2,1)}, bf16[1,2,1,256,256]{4,3,1,2,0:T(8,128)(2,1)S(1)}, u32[]{:S(2)}, u32[]{:S(2)}) collective-permute-start(bf16[1,2,1,256,256]{4,3,1,2,0:T(8,128)(2,1)} %bitcast.47), channel_id=1, source_target_pairs={{0,2},{2,0},{4,6},{6,4},{8,10},{10,8},{12,14},{14,12},{1,3},{3,1},... | collective-permute-start | bytes 786440 | tf_op jit(solution)/shard_map/ppermute | solution.py:18
  3.7 6.5 %collective-permute-done.1 = bf16[1,2,1,256,256]{4,3,1,2,0:T(8,128)(2,1)S(1)} collective-permute-done((bf16[1,2,1,256,256]{4,3,1,2,0:T(8,128)(2,1)}, bf16[1,2,1,256,256]{4,3,1,2,0:T(8,128)(2,1)S(1)}, u32[]{:S(2)}, u32[]{:S(2)}) %collective-permute-start.1) | collective-permute-done | bytes 262176 | tf_op jit(solution)/shard_map/ppermute | solution.py:18
  10.2 1.0 pad_maximum_fusion.3
  11.2 0.1 fusion.18
  11.4 1.9 %collective-permute-start.2 = (bf16[2,2,1,256,256]{4,3,1,0,2:T(8,128)(2,1)S(1)}, bf16[2,2,1,256,256]{4,3,1,0,2:T(8,128)(2,1)S(1)}, u32[]{:S(2)}, u32[]{:S(2)}) collective-permute-start(bf16[2,2,1,256,256]{4,3,1,0,2:T(8,128)(2,1)S(1)} %get-tuple-element.7), channel_id=1, source_target_pairs={{0,4},{2,6},{4,0},{6,2},{8,12},{10,14},{12,8},{14,10},{1,5},{3,7},... | collective-permute-start | bytes 1572872 | tf_op jit(solution)/shard_map/ppermute | solution.py:18
  13.2 0.0 collective-permute-start
  13.2 11.3 %collective-permute-done.2 = bf16[2,2,1,256,256]{4,3,1,0,2:T(8,128)(2,1)S(1)} collective-permute-done((bf16[2,2,1,256,256]{4,3,1,0,2:T(8,128)(2,1)S(1)}, bf16[2,2,1,256,256]{4,3,1,0,2:T(8,128)(2,1)S(1)}, u32[]{:S(2)}, u32[]{:S(2)}) %collective-permute-start.2) | collective-permute-done | bytes 524320 | tf_op jit(solution)/shard_map/ppermute | solution.py:18
  24.5 0.0 copy-start.2
  24.5 0.1 pad_maximum_fusion.2
  24.6 0.2 reverse_select_fusion.1
  24.8 2.6 %collective-permute-start.3 = (bf16[4,2,1,256,256]{4,3,1,0,2:T(8,128)(2,1)S(1)}, bf16[4,2,1,256,256]{4,3,1,0,2:T(8,128)(2,1)S(1)}, u32[]{:S(2)}, u32[]{:S(2)}) collective-permute-start(bf16[4,2,1,256,256]{4,3,1,0,2:T(8,128)(2,1)S(1)} %bitcast.43), channel_id=1, source_target_pairs={{0,8},{2,10},{4,12},{6,14},{8,0},{10,2},{12,4},{14,6},{1,9},{3,11}... | collective-permute-start | bytes 3145736 | tf_op jit(solution)/shard_map/ppermute | solution.py:18
  27.4 0.0 copy-done.2
  27.4 0.1 reshape.69
  27.5 0.0 copy-done
  27.5 0.7 gather_fusion
  28.2 0.1 reshape.68
  28.3 0.2 compare_reduce_fusion
  28.5 43.2 %collective-permute-done.3 = bf16[4,2,1,256,256]{4,3,1,0,2:T(8,128)(2,1)S(1)} collective-permute-done((bf16[4,2,1,256,256]{4,3,1,0,2:T(8,128)(2,1)S(1)}, bf16[4,2,1,256,256]{4,3,1,0,2:T(8,128)(2,1)S(1)}, u32[]{:S(2)}, u32[]{:S(2)}) %collective-permute-start.3) | collective-permute-done | bytes 1048608 | tf_op jit(solution)/shard_map/ppermute | solution.py:18
  71.7 0.2 pad_maximum_fusion.1
  71.9 0.5 reverse_select_fusion
  72.4 1.4 %fusion.2 = f32[2,2,256,256]{3,1,2,0:T(2,128)S(1)} fusion(bf16[8,2,1,256,256]{4,3,1,0,2:T(8,128)(2,1)S(1)} %bitcast.40, s32[2,8]{1,0:T(2,128)S(1)} %reshape.68, s32[2]{0:T(128)S(1)} %iota_add_fusion), kind=kOutput, calls=%fused_computation.8 | convolution fusion | flops 4194336 | bytes 3145800 | tf_op jit(solution)/shard_map/sik,skxw->sixw/dot_general | solution.py:35
  73.9 0.0 collective-permute-done
  73.9 2.5 %broadcast_select_fusion.1 = (bf16[2,8,256,256]{3,2,1,0:T(8,128)(2,1)S(1)}, bf16[2,8,256,256]{3,2,1,0:T(8,128)(2,1)S(1)}) fusion(bf16[2,8,256,256]{3,2,1,0:T(8,128)(2,1)} %param.5, bf16[2,8,256,256]{3,2,1,0:T(8,128)(2,1)} %collective-permute-done, pred[]{:T(512)S(6)} %eq.29), kind=kLoop, calls=%fused_computation.14 | loop fusion | flops 2097152 | bytes 8388609 | tf_op jit(solution)/shard_map/jit(_where)/select_n | solution.py:52
  76.4 2.3 %pad_maximum_fusion = bf16[2,16,256,256]{3,2,1,0:T(8,128)(2,1)} fusion(bf16[2,8,256,256]{3,2,1,0:T(8,128)(2,1)S(1)} %get-tuple-element.3, bf16[2,8,256,256]{3,2,1,0:T(8,128)(2,1)S(1)} %get-tuple-element.2), kind=kLoop, calls=%fused_computation.2 | loop fusion | flops 2097152 | bytes 8388608 | tf_op jit(solution)/shard_map/concatenate | solution.py:54
  78.7 5.0 %gather_fusion.1 = bf16[16,2,256,256]{3,2,1,0:T(8,128)(2,1)} fusion(bf16[2,16,256,256]{3,2,1,0:T(8,128)(2,1)} %pad_maximum_fusion, s32[1024]{0:T(1024)S(1)} %pad_clamp_fusion), kind=kCustom, calls=%fused_computation.1 | custom fusion | bytes 8388672 | tf_op jit(solution)/shard_map/jit(_take)/gather | solution.py:55
  83.6 0.0 copy-start.1
  83.6 4.3 %fusion.16 = (f32[2,256]{1,0:T(2,128)S(1)}, bf16[2,2,256,256]{3,2,1,0:T(8,128)(2,1)}) fusion(f32[2,2,256,256]{3,1,2,0:T(2,128)S(1)} %fusion.2, bf16[2,8,256,256,1]{3,2,0,1,4:T(8,128)(2,1)S(1)} %bitcast.41, bf16[2,2,8,256,256]{4,3,0,2,1:T(8,128)(2,1)} %bitcast.42, pred[2,8]{1,0:T(4,128)(4,1)S(1)} %compare_and_fusion, pred[2,2]{1,0:T(4,128)(4,1)S(1)} %compare_reduce_fusion), kind=kOutput, calls=%fused_computation.21 | convolution fusion | flops 1077149184 | bytes 7866388 | tf_op jit(solution)/shard_map/iskxy,skyw->sixw/dot_general | solution.py:34
  88.0 21.2 %psum.7 = f32[2,256]{1,0:T(2,128)S(1)} all-reduce(f32[2,256]{1,0:T(2,128)S(1)} %get-tuple-element.4), channel_id=1, replica_groups=mesh['fields'=2,'prow'=8,'pcol'=2] {'prow'}, use_global_device_ids=true, to_apply=%region_2.3 | all-reduce | flops 512 | bytes 4096 | tf_op jit(solution)/shard_map/psum | solution.py:60
  109.2 0.0 copy-done.1
  109.2 0.6 sub.3
  (6 shorter events, 0.0 us)
Async XLA Ops:
  0.6 26.9 %copy-start = (s32[16]{0:T(128)S(1)}, s32[16]{0:T(128)}, u32[]{:S(2)}) copy-start(s32[16]{0:T(128)} %param.9) | copy-start | bytes 196
  0.6 9.6 %collective-permute-start.1 = (bf16[1,2,1,256,256]{4,3,1,2,0:T(8,128)(2,1)}, bf16[1,2,1,256,256]{4,3,1,2,0:T(8,128)(2,1)S(1)}, u32[]{:S(2)}, u32[]{:S(2)}) collective-permute-start(bf16[1,2,1,256,256]{4,3,1,2,0:T(8,128)(2,1)} %bitcast.47), channel_id=1, source_target_pairs={{0,2},{2,0},{4,6},{6,4},{8,10},{10,8},{12,14},{14,12},{1,3},{3,1},... | collective-permute-start | bytes 786440 | tf_op jit(solution)/shard_map/ppermute | solution.py:18
  11.4 13.2 %collective-permute-start.2 = (bf16[2,2,1,256,256]{4,3,1,0,2:T(8,128)(2,1)S(1)}, bf16[2,2,1,256,256]{4,3,1,0,2:T(8,128)(2,1)S(1)}, u32[]{:S(2)}, u32[]{:S(2)}) collective-permute-start(bf16[2,2,1,256,256]{4,3,1,0,2:T(8,128)(2,1)S(1)} %get-tuple-element.7), channel_id=1, source_target_pairs={{0,4},{2,6},{4,0},{6,2},{8,12},{10,14},{12,8},{14,10},{1,5},{3,7},... | collective-permute-start | bytes 1572872 | tf_op jit(solution)/shard_map/ppermute | solution.py:18
  13.2 60.7 %collective-permute-start = (bf16[2,8,256,256]{3,2,1,0:T(8,128)(2,1)}, bf16[2,8,256,256]{3,2,1,0:T(8,128)(2,1)}, u32[]{:S(2)}, u32[]{:S(2)}) collective-permute-start(bf16[2,8,256,256]{3,2,1,0:T(8,128)(2,1)} %param.5), channel_id=1, source_target_pairs={{0,1},{1,0},{2,3},{3,2},{4,5},{5,4},{6,7},{7,6},{8,9},{9,8},{10,11... | collective-permute-start | bytes 6291464 | tf_op jit(solution)/shard_map/ppermute | solution.py:30
  24.5 2.9 %copy-start.2 = (s32[2,8]{1,0:T(2,128)S(1)}, s32[2,8]{1,0:T(2,128)}, u32[]{:S(2)}) copy-start(s32[2,8]{1,0:T(2,128)} %param.8) | copy-start | bytes 196
  24.8 46.9 %collective-permute-start.3 = (bf16[4,2,1,256,256]{4,3,1,0,2:T(8,128)(2,1)S(1)}, bf16[4,2,1,256,256]{4,3,1,0,2:T(8,128)(2,1)S(1)}, u32[]{:S(2)}, u32[]{:S(2)}) collective-permute-start(bf16[4,2,1,256,256]{4,3,1,0,2:T(8,128)(2,1)S(1)} %bitcast.43), channel_id=1, source_target_pairs={{0,8},{2,10},{4,12},{6,14},{8,0},{10,2},{12,4},{14,6},{1,9},{3,11}... | collective-permute-start | bytes 3145736 | tf_op jit(solution)/shard_map/ppermute | solution.py:18
  83.6 25.5 %copy-start.1 = (f32[2,256]{1,0:T(2,128)S(1)}, f32[2,256]{1,0:T(2,128)}, u32[]{:S(2)}) copy-start(f32[2,256]{1,0:T(2,128)} %param.7) | copy-start | bytes 6148
